TPU v7x, 32 devices: a whole 2x2x4 slice. The times are simulated.
32 devices in a mesh: parts: 2 (over y), att: 4 (over x, core), ffn: 4 (over z).
Axes of the slice: x: 2, y: 2, z: 4, core: 2. Of those that a mesh axis runs over, the one named last changes fastest.
Arguments:
- incoming: bfloat16 [128, 2, 8192], P('parts', None, 'att'), parts along dimension 0, may hold values from -60 to 60
- queries: bfloat16 [128, 2, 8192], P(('parts', 'att'), None, 'ffn'), parts along dimension 0, may hold values from -19 to 19
- new_kv: bfloat16 [128, 2, 2048], P(('parts', 'att'), None, 'ffn'), parts along dimension 0, may hold values from -6 to 6
- cache: bfloat16 [128, 640, 2048], P(('parts', 'att'), None, 'ffn'), parts along dimension 0, may hold values from -6 to 6
- lengths: int32 [128], P(('parts', 'att')), parts along dimension 0, may hold values from 1 to 640, 20480 in all
- slot_of: int32 [128], P('parts'), parts along dimension 0, may hold values from 0 to 63, each once
- w_out: bfloat16 [8192, 8192], P('ffn', 'att'), may hold values from -0.0625 to 0.0625
- norm_gain: float32 [8192], P('att'), may hold values from 0.5 to 1.5
- w_gate: bfloat16 [8192, 14336], P('att', 'ffn'), may hold values from -0.0625 to 0.0625
- w_up: bfloat16 [8192, 14336], P('att', 'ffn'), may hold values from -0.0625 to 0.0625
- w_down: bfloat16 [14336, 8192], P('ffn', 'att'), may hold values from -0.046875 to 0.046875
Outputs:
- out: bfloat16 [128, 2, 8192], P(('parts', 'ffn'), None, 'att'), parts along dimension 0
There are 2 independent parts, one for each index of `parts`. A program takes and returns all parts, laid end to end along the dimension named above; an argument that names none is the same for every part. Nothing has to cross between parts.
Inputs may be any that keep to these rules, and one draw needn't show every extreme that they name: In each part, the kept lengths of that part's 64 slots sum to 20480. `slot_of`: in each part, every slot holds exactly one request.
All inputs are finite; a program needn't handle non-finite values. No bound on the sum of `lengths` on one device may be relied on, other than what follows from the above.
Results may differ from a plain program's by a relative error of at most 0.0095.
Values may be sent and summed in bfloat16 or wider, within the bound.
A program may use at most 128 MiB of HBM per device.

v0:
```python
import jax
import jax.numpy as jnp
from jax import lax
from jax.sharding import PartitionSpec as P

D = 8192
H = 64
KVH = 8
HD = 128
STEPS = 2
CAP = 640


epsilon = 1e-05


def local(
    incoming, queries, new_kv, cache, lengths, slot_of, w_out, norm_gain, w_gate, w_up, w_down
):
    ffn_count = lax.axis_size("ffn")
    att_index = lax.axis_index("att")
    ffn_index = lax.axis_index("ffn")
    request_count = slot_of.shape[0]
    slot_count = cache.shape[0]
    kv_local = cache.shape[2] // (2 * HD)
    groups = H // KVH
    score_scale = HD ** (-0.5)
    gathered_q, gathered_kv = (
        lax.all_gather(queries, "att", axis=0, tiled=True),
        lax.all_gather(new_kv, "att", axis=0, tiled=True),
    )
    holders = (
        jnp.zeros((request_count,), jnp.int32)
        .at[slot_of]
        .set(jnp.arange(request_count, dtype=jnp.int32))
    )
    my_requests = lax.dynamic_slice_in_dim(holders, att_index * slot_count, slot_count)
    query_mine = jnp.take(gathered_q, my_requests, axis=0).reshape(
        slot_count, STEPS, kv_local, groups, HD
    )
    fresh_mine = jnp.take(gathered_kv, my_requests, axis=0).reshape(
        slot_count, STEPS, kv_local, 2, HD
    )
    cache_view = cache.reshape(slot_count, CAP, kv_local, 2, HD)
    fresh_scores = (
        jnp.einsum(
            "rskgd,rtkd->rskgt",
            query_mine,
            fresh_mine[:, :, :, 0],
            preferred_element_type=jnp.float32,
        )
        * score_scale
    )
    causal = jnp.arange(STEPS)[None, :] <= jnp.arange(STEPS)[:, None]
    fresh_scores = jnp.where(causal[None, :, None, None, :], fresh_scores, -jnp.inf)
    kept_scores = (
        jnp.einsum(
            "rskgd,rckd->rskgc",
            query_mine,
            cache_view[:, :, :, 0],
            preferred_element_type=jnp.float32,
        )
        * score_scale
    )
    in_range = jnp.arange(CAP)[None, :] < lengths[:, None]
    kept_scores = jnp.where(in_range[:, None, None, None, :], kept_scores, -jnp.inf)
    top_score = jnp.maximum(jnp.max(kept_scores, -1), jnp.max(fresh_scores, -1))
    kept_exp = jnp.exp(kept_scores - top_score[..., None])
    fresh_exp = jnp.exp(fresh_scores - top_score[..., None])
    denominator = jnp.sum(kept_exp, -1) + jnp.sum(fresh_exp, -1)
    kept_prob = (kept_exp / denominator[..., None]).astype(jnp.bfloat16)
    fresh_prob = (fresh_exp / denominator[..., None]).astype(jnp.bfloat16)
    mixture = jnp.einsum(
        "rskgc,rckd->rskgd", kept_prob, cache_view[:, :, :, 1], preferred_element_type=jnp.float32
    )
    mixture = mixture + jnp.einsum(
        "rskgt,rtkd->rskgd", fresh_prob, fresh_mine[:, :, :, 1], preferred_element_type=jnp.float32
    )
    attended = mixture.astype(jnp.bfloat16).reshape(slot_count, STEPS, kv_local * groups * HD)
    shard_rows = lax.all_gather(attended, "att", axis=0, tiled=True)
    row_count = shard_rows.shape[0]
    flattened = shard_rows.reshape(row_count * STEPS, shard_rows.shape[2])
    heads_slots = jnp.dot(flattened, w_out, preferred_element_type=jnp.float32).reshape(
        row_count, STEPS, w_out.shape[1]
    )
    heads_requests = jnp.take(heads_slots, slot_of, axis=0)
    heads_total = lax.psum(heads_requests, "ffn")
    residual = (incoming.astype(jnp.float32) + heads_total).astype(jnp.bfloat16)
    residual_wide = residual.astype(jnp.float32)
    squares = lax.psum(jnp.sum(residual_wide * residual_wide, -1), "att")
    normed = (residual_wide * lax.rsqrt(squares / D + epsilon)[..., None] * norm_gain).astype(
        jnp.bfloat16
    )
    normed = normed.reshape(request_count * STEPS, normed.shape[2])
    gate_term = jnp.dot(normed, w_gate, preferred_element_type=jnp.float32)
    upward_term = jnp.dot(normed, w_up, preferred_element_type=jnp.float32)
    unit_share = lax.psum_scatter(
        jnp.concatenate([gate_term, upward_term], 1), "att", scatter_dimension=0, tiled=True
    )
    unit_width = w_gate.shape[1]
    hidden_share = (jax.nn.silu(unit_share[:, :unit_width]) * unit_share[:, unit_width:]).astype(
        jnp.bfloat16
    )
    down_part = jnp.dot(
        lax.all_gather(hidden_share, "att", axis=0, tiled=True),
        w_down,
        preferred_element_type=jnp.float32,
    )
    out_share = lax.psum_scatter(down_part, "ffn", scatter_dimension=0, tiled=True)
    row_share = request_count // ffn_count
    own_state = lax.dynamic_slice_in_dim(residual_wide, ffn_index * row_share, row_share, 0)
    return (own_state + out_share.reshape(row_share, STEPS, out_share.shape[1])).astype(
        jnp.bfloat16
    )


def solution(mesh):
    return jax.shard_map(
        local,
        mesh=mesh,
        in_specs=(
            P("parts", None, "att"),
            P(("parts", "att"), None, "ffn"),
            P(("parts", "att"), None, "ffn"),
            P(("parts", "att"), None, "ffn"),
            P(("parts", "att")),
            P("parts"),
            P("ffn", "att"),
            P("att"),
            P("att", "ffn"),
            P("att", "ffn"),
            P("ffn", "att"),
        ),
        out_specs=P(("parts", "ffn"), None, "att"),
        check_vma=False,
    )
```

profile of v0, /device:TPU:0, one launch (start us, length us, event | category | flops | bytes accessed | tf_op | source)
XLA Modules:
  0.0 239.7 jit_solution(1182841661262097621)
XLA Ops:
  8.8 6.7 %all_gather.13 = bf16[64,2,512]{2,1,0:T(2,128)(2,1)S(1)} all-gather(bf16[16,2,512]{2,1,0:T(2,128)(2,1)} %param.13), channel_id=1, replica_groups=mesh['parts'=2,'att'=4,'ffn'=4] {'att'}, dimensions={0}, use_global_device_ids=true | all-gather | bytes 163840 | tf_op jit(solution)/shard_map/all_gather | solution.py:30
  16.1 7.8 %all_gather.12 = bf16[64,2,2048]{2,1,0:T(2,128)(2,1)S(1)} all-gather(bf16[16,2,2048]{2,1,0:T(2,128)(2,1)} %param.12), channel_id=1, replica_groups=mesh['parts'=2,'att'=4,'ffn'=4] {'att'}, dimensions={0}, use_global_device_ids=true | all-gather | bytes 655360 | tf_op jit(solution)/shard_map/all_gather | solution.py:29
  24.8 14.8 %copy.41 = bf16[16,640,512]{1,2,0:T(8,128)(2,1)} copy(bf16[16,640,512]{2,1,0:T(8,128)(2,1)} %param.14) | data formatting | bytes 20971520 | tf_op args[3]
  40.6 3.6 %bitcast_reduce_fusion = (f32[16,2,2,8]{3,1,2,0:T(2,128)S(1)}, f32[16,2,2,8,640]{4,3,2,1,0:T(8,128)S(1)}) fusion(bf16[16,640,2,2,128]{1,4,3,2,0:T(8,128)(2,1)} %bitcast.75, bf16[16,2,2,8,128]{4,3,2,1,0:T(8,128)(2,1)S(1)} %gather.17, pred[16]{0:T(512)(128)(4,1)S(1)} %get-tuple-element.7, pred[16,640]{1,0:T(8,128)(4,1)S(1)} %iota_compare_fusion), kind=kOutput, calls=%fused_computation.13 | convolution fusion | flops 84934144 | bytes 6696976 | tf_op jit(solution)/shard_map/rskgd,rckd->rskgc/dot_general | solution.py:57
  44.8 4.3 %fusion.7 = f32[16,2,2,8,128]{4,3,1,2,0:T(8,128)S(1)} fusion(bf16[16,640,2,2,128]{1,4,3,2,0:T(8,128)(2,1)} %bitcast.76, f32[16,2,2,8,640]{4,3,2,1,0:T(8,128)S(1)} %get-tuple-element.10, f32[16,2,2,8]{3,1,2,0:T(2,128)S(1)} %add.60, f32[16,2,2,8]{3,1,2,0:T(2,128)S(1)} %max.7), kind=kOutput, calls=%fused_computation.17 | convolution fusion | flops 84869120 | bytes 6819840 | tf_op jit(solution)/shard_map/rskgc,rckd->rskgd/dot_general | solution.py:73
  49.5 7.3 %all_gather.14 = bf16[64,2,2048]{2,0,1:T(8,128)(2,1)S(1)} all-gather(bf16[16,2,2048]{2,0,1:T(8,128)(2,1)S(1)} %reshape.72), channel_id=1, replica_groups=mesh['parts'=2,'att'=4,'ffn'=4] {'att'}, dimensions={0}, use_global_device_ids=true | all-gather | bytes 655360 | tf_op jit(solution)/shard_map/all_gather | solution.py:80
  56.8 4.7 %fusion = f32[64,2,2048]{2,0,1:T(8,128)S(1)} fusion(bf16[64,2,2048]{2,0,1:T(8,128)(2,1)S(1)} %all_gather.14, bf16[2048,2048]{1,0:T(8,128)(2,1)} %param.17), kind=kOutput, calls=%fused_computation.4 | convolution fusion | flops 1073741824 | bytes 9961472 | tf_op jit(solution)/shard_map/dot_general | solution.py:83
  62.3 1.7 gather_fusion.2
  64.0 1.6 broadcast_select_fusion
  65.6 53.4 %all-reduce.2.cloned.1.call-done = f32[64,2,2048]{2,1,0:T(2,128)} async-done(((f32[64,2,2048]{2,1,0:T(2,128)}), f32[64,2,2048]{2,1,0:T(2,128)}) %all-reduce.2.cloned.1.call-update) | async-done | bytes 1048592 | tf_op jit(solution)/shard_map/psum | solution.py:87
  119.0 2.3 multiply_reduce_fusion
  121.3 7.0 %psum.15 = f32[64,2]{0,1:T(2,128)S(1)} all-reduce(f32[64,2]{0,1:T(2,128)S(1)} %copy.48), channel_id=1, replica_groups=mesh['parts'=2,'att'=4,'ffn'=4] {'att'}, use_global_device_ids=true, to_apply=%region_7.8 | all-reduce | flops 128 | bytes 1024 | tf_op jit(solution)/shard_map/psum | solution.py:90
  128.4 1.3 multiply_convert_fusion
  129.7 1.2 reshape.73
  131.0 7.4 %fusion.26 = f32[128,3584]{1,0:T(8,128)S(1)} fusion(bf16[128,2048]{1,0:T(8,128)(2,1)S(1)} %reshape.73, bf16[2048,3584]{1,0:T(8,128)(2,1)} %param.19), kind=kOutput, calls=%fused_computation.58 | convolution fusion | flops 1879048192 | bytes 17039360 | tf_op jit(solution)/shard_map/dot_general | solution.py:95
  138.6 1.2 slice-done.3
  139.8 2.1 fusion.27
  141.9 2.0 pad_maximum_fusion
  144.0 39.7 %reduce-scatter.3.cloned.1.call-done = f32[32,7168]{1,0:T(8,128)} async-done(((f32[128,7168]{1,0:T(8,128)}), f32[32,7168]{1,0:T(8,128)}) %reduce-scatter.3.cloned.1.call-update) | async-done | bytes 917520 | tf_op jit(solution)/shard_map/reduce_scatter | solution.py:97
  183.7 1.3 fusion.16
  185.0 8.7 %all_gather.15 = bf16[128,3584]{1,0:T(8,128)(2,1)S(1)} all-gather(bf16[32,3584]{1,0:T(8,128)(2,1)S(1)} %fusion.16), channel_id=1, replica_groups=mesh['parts'=2,'att'=4,'ffn'=4] {'att'}, dimensions={0}, use_global_device_ids=true | all-gather | bytes 1146880 | tf_op jit(solution)/shard_map/all_gather | solution.py:105
  193.7 8.5 %fusion.28 = f32[128,2048]{1,0:T(8,128)} fusion(bf16[128,3584]{1,0:T(8,128)(2,1)S(1)} %all_gather.15, bf16[3584,2048]{1,0:T(8,128)(2,1)} %param.21), kind=kOutput, calls=%fused_computation.60 | convolution fusion | flops 1879048192 | bytes 16646144 | tf_op jit(solution)/shard_map/dot_general | solution.py:104
  202.3 28.0 %reduce-scatter.5.cloned.1.call-done = f32[32,2048]{1,0:T(8,128)} async-done(((f32[128,2048]{1,0:T(8,128)}), f32[32,2048]{1,0:T(8,128)}) %reduce-scatter.5.cloned.1.call-update) | async-done | bytes 262160 | tf_op jit(solution)/shard_map/reduce_scatter | solution.py:109
  231.4 1.8 add_convert_fusion.1
  (47 shorter events, 8.1 us)
Async XLA Ops:
  6.5 112.4 %all-reduce.2.cloned.1.call-start = ((), (), s32[]{:S(2)}) async-start(), calls=%async_computation.2 | async-start | bytes 2097152 | tf_op jit(solution)/shard_map/psum | solution.py:87
  24.8 14.8 %copy-start.2 = (s32[16]{0:T(128)S(1)}, s32[16]{0:T(128)}, u32[]{:S(2)}) copy-start(s32[16]{0:T(128)} %param.15) | copy-start | bytes 196
  62.3 66.1 %copy-start.1 = (f32[2048]{0:T(1024)S(1)}, f32[2048]{0:T(1024)}, u32[]{:S(2)}) copy-start(f32[2048]{0:T(1024)} %param.18) | copy-start | bytes 24580
  65.5 118.2 %reduce-scatter.3.cloned.1.call-start = ((), (), s32[]{:S(2)}) async-start(), calls=%async_computation.3 | async-start | bytes 4587520 | tf_op jit(solution)/shard_map/reduce_scatter | solution.py:97
  119.0 19.5 %slice-start = ((s8[14680064]{0:T(1024)(128)(4,1)}), s8[2097152]{0:T(1024)(128)(4,1)S(1)}, s32[]{:S(2)}) async-start(s8[14680064]{0:T(1024)(128)(4,1)} %bitcast.73), calls=%async_computation.5 | async-start | bytes 4194304
  121.2 7.2 %copy-start = (f32[64,2,2048]{2,1,0:T(2,128)}, f32[64,2,2048]{2,1,0:T(2,128)S(1)}, u32[]{:S(2)}) copy-start(f32[64,2,2048]{2,1,0:T(2,128)S(1)} %get-tuple-element.6) | copy-start | bytes 3145732
  131.0 7.5 %slice-start.1 = ((s8[14680064]{0:T(1024)(128)(4,1)}), s8[4194304]{0:T(1024)(128)(4,1)S(1)}, s32[]{:S(2)}) async-start(s8[14680064]{0:T(1024)(128)(4,1)} %bitcast.73), calls=%async_computation.6 | async-start | bytes 8388608
  131.0 7.6 %slice-start.2 = ((s8[14680064]{0:T(1024)(128)(4,1)}), s8[4194304]{0:T(1024)(128)(4,1)S(1)}, s32[]{:S(2)}) async-start(s8[14680064]{0:T(1024)(128)(4,1)} %bitcast.73), calls=%async_computation.7 | async-start | bytes 8388608
  131.0 8.8 %slice-start.3 = ((s8[14680064]{0:T(1024)(128)(4,1)}), s8[4194304]{0:T(1024)(128)(4,1)S(1)}, s32[]{:S(2)}) async-start(s8[14680064]{0:T(1024)(128)(4,1)} %bitcast.73), calls=%async_computation.8 | async-start | bytes 8388608
  144.0 86.3 %reduce-scatter.5.cloned.1.call-start = ((), (), s32[]{:S(2)}) async-start(), calls=%async_computation.4 | async-start | bytes 1310720 | tf_op jit(solution)/shard_map/reduce_scatter | solution.py:109
Sparse Core Ops, SparseCore 0:
  65.7 53.2 all-reduce.1
  144.1 39.5 reduce-scatter.2
  202.4 27.8 reduce-scatter.4
where the time goes:
time: 240 us
  waiting for transfers between devices  121 us (50%)
  blocking collectives  37.5 us (16%)
  matrix products  31.6 us (13%)
  local copies, waits for them, and re-layouts  23.6 us (10%)
  between operations  13.3 us (6%)
  other arithmetic  12.4 us (5%)
    psum x1, waiting for transfers between devices, local(): heads_total = lax.psum(heads_requests, 'ffn')  53.4 us
    reduce_scatter x1, waiting for transfers between devices, local(): lax.psum_scatter(jnp.concatenate([gate_term, upward_term], 1), 'att', sca...  39.7 us
    reduce_scatter x1, waiting for transfers between devices, local(): lax.psum_scatter(down_part, 'ffn', scatter_dimension=0, tiled=True)  28 us
    unnamed x15, local copies, waits for them, and re-layouts  16.2 us
    all_gather x1, blocking collectives, local(): lax.all_gather(hidden_share, 'att', axis=0, tiled=True)  8.73 us
    dot_general x1, matrix products, local(): jnp.dot(lax.all_gather(hidden_share, 'att', axis=0, tiled=True), w_down,...  8.51 us
    all_gather x1, blocking collectives, local(): lax.all_gather(queries, 'att', axis=0, tiled=True)  7.77 us
    dot_general x1, matrix products, local(): gate_term = jnp.dot(normed, w_gate, preferred_element_type=jnp.float32)  7.4 us
  transfers between devices with their start and end apart: 3, of which 3 were waited for; matrix products, arithmetic and copies ran while one was open for 0% of the time, Pallas kernels for 0%

commit v1 on v0

--- a/solution.py
+++ b/solution.py
@@ -1,6 +1,10 @@
+import functools
+
 import jax
 import jax.numpy as jnp
 from jax import lax
+from jax.experimental import pallas as pl
+from jax.experimental.pallas import tpu as pltpu
 from jax.sharding import PartitionSpec as P
 
 D = 8192
@@ -12,12 +16,254 @@
 
 
 epsilon = 1e-05
+TILE = 512
+MESH = pl.DeviceIdType.MESH
+
+
+def tail_kernel(
+    cfg, attended, incoming, gain, wo, wg, wu, wd, out,
+    wo_v, wg_v, wu_v, wd_v,
+    fa, pa, oa, ra, res, h, ss, ssr,
+    fg, s1, o1, r1, s2, o2, r2, hb,
+    pd, od, rd,
+    wo_s, wg_s, wu_s, wd_s,
+    a_ss, a_rs, b_ss, b_rs, q_ss, q_rs,
+    c1_ss, c1_rs, c2_ss, c2_rs,
+    hp_ss, hp_rs, hx_ss, hx_rs, hf_ss, hf_rs,
+    d_ss, d_rs,
+):
+    Z, RB, T, NA, NF = cfg
+    A = 4
+    z = lax.axis_index("ffn")
+    a = lax.axis_index("att")
+    x, c = a // 2, a % 2
+    partner = 2 * x + (1 - c)
+    xpeer = 2 * (1 - x) + c
+    bf, f32 = jnp.bfloat16, jnp.float32
+
+    def wcopy(src, dst, sem, k):
+        return pltpu.make_async_copy(
+            src.at[:, pl.ds(pl.multiple_of(k * T, T), T)], dst.at[k], sem.at[k]
+        )
+
+    for k in range(NA):
+        wcopy(wo, wo_v, wo_s, k).start()
+    for k in range(NF):
+        wcopy(wg, wg_v, wg_s, k).start()
+        wcopy(wu, wu_v, wu_s, k).start()
+    for k in range(NA):
+        wcopy(wd, wd_v, wd_s, k).start()
+
+    barrier = pltpu.get_barrier_semaphore()
+    for d in range(1, Z):
+        pl.semaphore_signal(barrier, 1, device_id={"ffn": (z + d) % Z}, device_id_type=MESH)
+    for d in range(1, A):
+        pl.semaphore_signal(barrier, 1, device_id={"att": (a + d) % A}, device_id_type=MESH)
+    pl.semaphore_wait(barrier, Z - 1 + A - 1)
+
+    def remote(src, dst, ss_, rs_, axis, peer):
+        return pltpu.make_async_remote_copy(
+            src_ref=src, dst_ref=dst, send_sem=ss_, recv_sem=rs_,
+            device_id={axis: peer}, device_id_type=MESH,
+        )
+
+    def a_copy(k, d):
+        peer = (z + d) % Z
+        return remote(pa.at[k, peer], ra.at[k, d - 1], a_ss.at[k, d - 1], a_rs.at[k, d - 1], "ffn", peer)
+
+    def b_copy(k, d):
+        peer = (z + d) % Z
+        return remote(res.at[k, z], res.at[k, z], b_ss.at[k, d - 1], b_rs.at[k, d - 1], "ffn", peer)
+
+    def b_wait(k, d):
+        origin = (z + Z - d) % Z
+        remote(res.at[k, origin], res.at[k, origin], b_ss.at[k, d - 1], b_rs.at[k, d - 1], "ffn", origin).wait_recv()
+
+    def q_copy(d):
+        peer = (a + d) % A
+        return remote(ss.at[peer], ssr.at[d - 1], q_ss.at[d - 1], q_rs.at[d - 1], "att", peer)
+
+    def c1_copy(k):
+        return remote(s1.at[k], r1.at[k], c1_ss.at[k], c1_rs.at[k], "att", partner)
+
+    def c2_copy(k):
+        return remote(s2.at[k], r2.at[k], c2_ss.at[k], c2_rs.at[k], "att", xpeer)
+
+    def hp_copy(k, block):
+        return remote(hb.at[k, block], hb.at[k, block], hp_ss.at[k], hp_rs.at[k], "att", partner)
+
+    def hx_copy(k, block):
+        return remote(hb.at[k, block], hb.at[k, block], hx_ss.at[k], hx_rs.at[k], "att", xpeer)
+
+    def hf_copy(k, block):
+        return remote(hb.at[k, block], hb.at[k, block], hf_ss.at[k], hf_rs.at[k], "att", partner)
+
+    def d_copy(k, d):
+        peer = (z + d) % Z
+        return remote(pd.at[k, peer], rd.at[k, d - 1], d_ss.at[k, d - 1], d_rs.at[k, d - 1], "ffn", peer)
+
+    @pl.loop(0, NA)
+    def _(k):
+        wcopy(wo, wo_v, wo_s, k).wait()
+        p = jnp.dot(attended[...], wo_v[k], preferred_element_type=f32).reshape(Z, RB, T)
+        fa[...] = p
+        pa[k] = p.astype(bf)
+        oa[k] = fa[z]
+        for d in range(1, Z):
+            a_copy(k, d).start()
+
+    for k in range(NA):
+        total = incoming[z, :, k * T:(k + 1) * T].astype(f32) + oa[k]
+        for d in range(1, Z):
+            a_copy(k, d).wait_recv()
+            total = total + ra[k, d - 1].astype(f32)
+        res[k, z] = total.astype(bf)
+        for d in range(1, Z):
+            b_copy(k, d).start()
+
+    squares = jnp.zeros((Z, RB, 1), f32)
+    for k in range(NA):
+        for d in range(1, Z):
+            b_wait(k, d)
+        wide = res[k].astype(f32)
+        squares = squares + jnp.sum(wide * wide, -1, keepdims=True)
+        h[:, k * T:(k + 1) * T] = (
+            (wide * gain[:, k * T:(k + 1) * T]).astype(bf).reshape(Z * RB, T)
+        )
+    ss[...] = jnp.broadcast_to(squares.reshape(A, ss.shape[1], 1), ss.shape)
+    for d in range(1, A):
+        q_copy(d).start()
+
+    def first(k):
+        wcopy(wg, wg_v, wg_s, k).wait()
+        wcopy(wu, wu_v, wu_s, k).wait()
+        for i, w in enumerate((wg_v, wu_v)):
+            p = jnp.dot(h[...], w[k], preferred_element_type=f32)
+            fg[i] = p.reshape(fg.shape[1:])
+            for xx in range(2):
+                s1[k, i, xx] = fg[i, 2 * xx + (1 - c)].astype(bf)
+                o1[k, i, xx] = fg[i, 2 * xx + c]
+        c1_copy(k).start()
+
+    def second(k):
+        c1_copy(k).wait_recv()
+        for i in range(2):
+            s2[k, i] = (o1[k, i, 1 - x] + r1[k, i, 1 - x].astype(f32)).astype(bf)
+            o2[k, i] = o1[k, i, x] + r1[k, i, x].astype(f32)
+        c2_copy(k).start()
+
+    first(0)
+
+    @pl.loop(1, NF)
+    def _(k):
+        first(k)
+        second(k - 1)
+
+    second(NF - 1)
+
+    total_squares = ss[a]
+    for d in range(1, A):
+        q_copy(d).wait_recv()
+        total_squares = total_squares + ssr[d - 1]
+    inverse = lax.rsqrt(total_squares / D + epsilon)[:, :1]
+
+    @pl.loop(0, NF)
+    def _(k):
+        c2_copy(k).wait_recv()
+        gate = (o2[k, 0] + r2[k, 0].astype(f32)) * inverse
+        up = (o2[k, 1] + r2[k, 1].astype(f32)) * inverse
+        hb[k, a] = (gate / (1.0 + jnp.exp(-gate)) * up).astype(bf)
+        hx_copy(k, a).start()
+        hp_copy(k, a).start()
+
+    @pl.loop(0, NF)
+    def _(k):
+        hx_copy(k, xpeer).wait_recv()
+        hf_copy(k, xpeer).start()
+
+    @pl.loop(0, NF)
+    def _(k):
+        hp_copy(k, partner).wait_recv()
+        hf_copy(k, 2 * (1 - x) + (1 - c)).wait_recv()
+
+    @pl.loop(0, NA)
+    def _(n):
+        wcopy(wd, wd_v, wd_s, n).wait()
+        p = jnp.zeros((Z * RB, T), f32)
+        for k in range(NF):
+            p = p + jnp.dot(
+                hb[k].reshape(Z * RB, T), wd_v[n, k * T:(k + 1) * T, :], preferred_element_type=f32
+            )
+        p = p.reshape(Z, RB, T)
+        fa[...] = p
+        pd[n] = p.astype(bf)
+        od[n] = fa[z]
+        for d in range(1, Z):
+            d_copy(n, d).start()
+
+    for n in range(NA):
+        total = res[n, z].astype(f32) + od[n]
+        for d in range(1, Z):
+            d_copy(n, d).wait_recv()
+            total = total + rd[n, d - 1].astype(f32)
+        out[:, n * T:(n + 1) * T] = total.astype(bf)
+
+    for k in range(NA):
+        for d in range(1, Z):
+            a_copy(k, d).wait_send()
+            b_copy(k, d).wait_send()
+            d_copy(k, d).wait_send()
+    for d in range(1, A):
+        q_copy(d).wait_send()
+    for k in range(NF):
+        c1_copy(k).wait_send()
+        c2_copy(k).wait_send()
+        hp_copy(k, a).wait_send()
+        hx_copy(k, a).wait_send()
+        hf_copy(k, xpeer).wait_send()
+
+
+def tail(attended, incoming, gain, w_out, w_gate, w_up, w_down):
+    Z = lax.axis_size("ffn")
+    rows, kdim = attended.shape
+    width = w_out.shape[1]
+    units = w_gate.shape[1]
+    RB, T = rows // Z, TILE
+    NA, NF = width // T, units // T
+    AB = rows // 4
+    bf, f32 = jnp.bfloat16, jnp.float32
+    V = pltpu.VMEM
+    dma = pltpu.SemaphoreType.DMA
+    vm = pl.BlockSpec(memory_space=pltpu.VMEM)
+    hbm = pl.BlockSpec(memory_space=pl.ANY)
+    scratch = [
+        V((NA, kdim, T), bf), V((NF, width, T), bf), V((NF, width, T), bf), V((NA, units, T), bf),
+        V((Z, RB, T), f32), V((NA, Z, RB, T), bf), V((NA, RB, T), f32), V((NA, Z - 1, RB, T), bf),
+        V((NA, Z, RB, T), bf), V((rows, width), bf), V((4, AB, 128), f32), V((3, AB, 128), f32),
+        V((2, 4, AB, T), f32), V((NF, 2, 2, AB, T), bf), V((NF, 2, 2, AB, T), f32),
+        V((NF, 2, 2, AB, T), bf), V((NF, 2, AB, T), bf), V((NF, 2, AB, T), f32),
+        V((NF, 2, AB, T), bf), V((NF, 4, AB, T), bf),
+        V((NA, Z, RB, T), bf), V((NA, RB, T), f32), V((NA, Z - 1, RB, T), bf),
+        dma((NA,)), dma((NF,)), dma((NF,)), dma((NA,)),
+        dma((NA, Z - 1)), dma((NA, Z - 1)), dma((NA, Z - 1)), dma((NA, Z - 1)), dma((3,)), dma((3,)),
+    ] + [dma((NF,)) for _ in range(10)] + [dma((NA, Z - 1)), dma((NA, Z - 1))]
+    return pl.pallas_call(
+        functools.partial(tail_kernel, (Z, RB, T, NA, NF)),
+        out_shape=jax.ShapeDtypeStruct((RB, width), bf),
+        in_specs=[vm, vm, vm, hbm, hbm, hbm, hbm],
+        out_specs=vm,
+        scratch_shapes=scratch,
+        compiler_params=pltpu.CompilerParams(
+            collective_id=1, has_side_effects=True, vmem_limit_bytes=67043328
+        ),
+    )(attended, incoming, gain, w_out, w_gate, w_up, w_down)
 
 
 def local(
     incoming, queries, new_kv, cache, lengths, slot_of, w_out, norm_gain, w_gate, w_up, w_down
 ):
     ffn_count = lax.axis_size("ffn")
+    fast = lax.axis_size("att") == 4 and slot_of.shape[0] * STEPS <= 128
     att_index = lax.axis_index("att")
     ffn_index = lax.axis_index("ffn")
     request_count = slot_of.shape[0]
@@ -80,6 +326,17 @@
     shard_rows = lax.all_gather(attended, "att", axis=0, tiled=True)
     row_count = shard_rows.shape[0]
     flattened = shard_rows.reshape(row_count * STEPS, shard_rows.shape[2])
+    if fast:
+        own = tail(
+            jnp.take(shard_rows, slot_of, axis=0).reshape(row_count * STEPS, -1),
+            incoming.reshape(ffn_count, -1, incoming.shape[2]),
+            norm_gain[None],
+            w_out,
+            w_gate,
+            w_up,
+            w_down,
+        )
+        return own.reshape(-1, STEPS, incoming.shape[2])
     heads_slots = jnp.dot(flattened, w_out, preferred_element_type=jnp.float32).reshape(
         row_count, STEPS, w_out.shape[1]
     )

time: 240 us -> 125 us (0.52)
  waiting for transfers between devices: 121 us -> 0 us
  Pallas kernels: 0 us -> 68.7 us
  matrix products: 31.6 us -> 8.92 us
  blocking collectives: 37.5 us -> 21.8 us
  between operations: 13.3 us -> 0.16 us
  other arithmetic: 12.4 us -> 2.46 us
    pallas_call x0 -> x1, Pallas kernels: none -> 68.7 us  [tail(): pl.pallas_call(functools.partial(tail_kernel, (Z, RB, T, NA, NF)), out_sh...]
    reduce_scatter x2 -> x0, waiting for transfers between devices: 67.7 us -> none  [the longest x1 39.7 us: local(): lax.psum_scatter(jnp.concatenate([gate_term, upward_term], 1), 'att', sca...]
    psum x1 -> x0, waiting for transfers between devices: 53.4 us -> none  [local(): heads_total = lax.psum(heads_requests, 'ffn')]
    dot_general x4 -> x0, matrix products: 22.6 us -> none  [the longest x1 8.51 us: local(): jnp.dot(lax.all_gather(hidden_share, 'att', axis=0, tiled=True), w_down,...]
    all_gather x1 -> x0, blocking collectives: 8.73 us -> none  [local(): lax.all_gather(hidden_share, 'att', axis=0, tiled=True)]
    psum x1 -> x0, blocking collectives: 7 us -> none  [local(): squares = lax.psum(jnp.sum(residual_wide * residual_wide, -1), 'att')]
    convert_element_type x3 -> x0, other arithmetic: 4.37 us -> none  [the longest x1 1.75 us: local(): (own_state + out_share.reshape(row_share, STEPS, out_share.shape[1])).ast...]
    unnamed x15 -> x7, local copies, waits for them, and re-layouts: 16.2 us -> 14.8 us
  transfers between devices with their start and end apart: 3 -> 0, of which waited for: 3 -> 0; matrix products, arithmetic and copies ran while one was open for 0% -> 0% of each run, Pallas kernels for 0% -> 0%
where the time goes in v1:
time: 125 us; the launch traced here: 124 us
  Pallas kernels  68.7 us (55%)
  local copies, waits for them, and re-layouts  21.9 us (18%)
  blocking collectives  21.8 us (17%)
  matrix products  8.92 us (7%)
  other arithmetic  2.46 us (2%)
    pallas_call x1, Pallas kernels, tail(): pl.pallas_call(functools.partial(tail_kernel, (Z, RB, T, NA, NF)), out_sh...  68.7 us
    unnamed x7, local copies, waits for them, and re-layouts  14.8 us
    all_gather x1, blocking collectives, local(): lax.all_gather(queries, 'att', axis=0, tiled=True)  7.77 us
    all_gather x1, blocking collectives, local(): shard_rows = lax.all_gather(attended, 'att', axis=0, tiled=True)  7.28 us
    all_gather x1, blocking collectives, local(): lax.all_gather(new_kv, 'att', axis=0, tiled=True)  6.72 us
    dot_general x1, matrix products, local(): jnp.einsum('rskgc,rckd->rskgd', kept_prob, cache_view[:, :, :, 1], prefer...  4.26 us
    dot_general x1, matrix products, local(): jnp.einsum('rskgd,rckd->rskgc', query_mine, cache_view[:, :, :, 0], prefe...  3.57 us

profile of v1, /device:TPU:0, one launch (start us, length us, event | category | flops | bytes accessed | tf_op | source)
XLA Modules:
  0.0 124.0 jit_solution(8459576203162058147)
XLA Ops:
  0.0 0.7 compare_select_fusion.1
  0.7 0.8 scatter_custom_fusion
  1.4 0.1 compare_and_fusion
  1.5 6.7 %all_gather.10 = bf16[64,2,512]{2,1,0:T(2,128)(2,1)S(1)} all-gather(bf16[16,2,512]{2,1,0:T(2,128)(2,1)} %param.13), channel_id=1, replica_groups=mesh['parts'=2,'att'=4,'ffn'=4] {'att'}, dimensions={0}, use_global_device_ids=true | all-gather | bytes 163840 | tf_op jit(solution)/shard_map/all_gather | solution.py:276
  8.3 0.6 gather_fusion.1
  8.9 0.1 broadcast_select_fusion.1
  9.0 7.8 %all_gather.9 = bf16[64,2,2048]{2,1,0:T(2,128)(2,1)S(1)} all-gather(bf16[16,2,2048]{2,1,0:T(2,128)(2,1)} %param.12), channel_id=1, replica_groups=mesh['parts'=2,'att'=4,'ffn'=4] {'att'}, dimensions={0}, use_global_device_ids=true | all-gather | bytes 655360 | tf_op jit(solution)/shard_map/all_gather | solution.py:275
  16.8 0.8 gather_fusion
  17.6 0.1 gather.19
  17.7 0.8 fusion.20
  18.5 14.8 %copy.30 = bf16[16,640,512]{1,2,0:T(8,128)(2,1)} copy(bf16[16,640,512]{2,1,0:T(8,128)(2,1)} %param.14) | data formatting | bytes 20971520 | tf_op args[3]
  33.4 3.6 %bitcast_reduce_fusion = (f32[16,2,2,8]{3,1,2,0:T(2,128)S(1)}, f32[16,2,2,8,640]{4,3,2,1,0:T(8,128)S(1)}) fusion(bf16[16,640,2,2,128]{1,4,3,2,0:T(8,128)(2,1)} %bitcast.62, bf16[16,2,2,8,128]{4,3,2,1,0:T(8,128)(2,1)S(1)} %gather.19, pred[16]{0:T(512)(128)(4,1)S(1)} %get-tuple-element.5, pred[16,640]{1,0:T(8,128)(4,1)S(1)} %iota_compare_fusion), kind=kOutput, calls=%fused_computation.10 | convolution fusion | flops 84934144 | bytes 6696976 | tf_op jit(solution)/shard_map/rskgd,rckd->rskgc/dot_general | solution.py:303
  37.0 0.1 fusion.13
  37.2 0.4 fusion.7
  37.6 4.3 %fusion.5 = f32[16,2,2,8,128]{4,3,1,2,0:T(8,128)S(1)} fusion(bf16[16,640,2,2,128]{1,4,3,2,0:T(8,128)(2,1)} %bitcast.63, f32[16,2,2,8,640]{4,3,2,1,0:T(8,128)S(1)} %get-tuple-element.8, f32[16,2,2,8]{3,1,2,0:T(2,128)S(1)} %add.33, f32[16,2,2,8]{3,1,2,0:T(2,128)S(1)} %max.7), kind=kOutput, calls=%fused_computation.14 | convolution fusion | flops 84869120 | bytes 6819840 | tf_op jit(solution)/shard_map/rskgc,rckd->rskgd/dot_general | solution.py:319
  41.9 0.3 fusion.8
  42.3 7.3 %all_gather.11 = bf16[64,2,2048]{2,1,0:T(2,128)(2,1)S(1)} all-gather(bf16[16,2,2048]{2,1,0:T(2,128)(2,1)S(1)} %reshape.113), channel_id=1, replica_groups=mesh['parts'=2,'att'=4,'ffn'=4] {'att'}, dimensions={0}, use_global_device_ids=true | all-gather | bytes 655360 | tf_op jit(solution)/shard_map/all_gather | solution.py:326
  49.6 1.6 %gather_fusion.2 = bf16[64,2,2048]{2,1,0:T(2,128)(2,1)S(1)} fusion(bf16[64,2,2048]{2,1,0:T(2,128)(2,1)S(1)} %all_gather.11, s32[1024]{0:T(1024)S(1)} %pad_clamp_fusion), kind=kCustom, calls=%fused_computation.2 | custom fusion | bytes 1048832 | tf_op jit(solution)/shard_map/jit(_take)/gather | solution.py:331
  51.2 0.2 gather.23
  51.5 0.2 broadcast_in_dim.77
  51.6 0.9 broadcast_select_fusion.attended
  52.6 1.0 reshape.70.incoming
  53.6 68.7 %shard_map.109 = bf16[32,2048]{1,0:T(8,128)(2,1)} custom-call(bf16[128,2048]{1,0:T(8,128)(2,1)} %broadcast_select_fusion.attended, bf16[4,32,2048]{2,1,0:T(8,128)(2,1)} %reshape.70.incoming, f32[1,2048]{1,0:T(1,128)} %bitcast.64, bf16[2048,2048]{1,0:T(8,128)(2,1)} %wo.1, bf16[2048,3584]{1,0:T(8,128)(2,1)} %wg.1, bf16[2048,3584]{1,0:T(8,128)(2,1)} %wu.1, ...), custom_call_target="tpu_custom_call" | custom-call | tf_op jit(solution)/shard_map/pallas_call | solution.py:250
  122.3 1.7 %reshape.71 = bf16[16,2,2048]{2,1,0:T(2,128)(2,1)} reshape(bf16[32,2048]{1,0:T(8,128)(2,1)} %shard_map.109) | data formatting | bytes 262144 | tf_op jit(solution)/shard_map/reshape | solution.py:339
  (18 shorter events, 0.3 us)
Async XLA Ops:
  18.5 14.8 %copy-start.1 = (s32[16]{0:T(128)S(1)}, s32[16]{0:T(128)}, u32[]{:S(2)}) copy-start(s32[16]{0:T(128)} %param.15) | copy-start | bytes 196
  42.3 9.1 %copy-start.2 = (s32[64]{0:T(128)S(1)}, s32[64]{0:T(128)}, u32[]{:S(2)}) copy-start(s32[64]{0:T(128)} %param.16) | copy-start | bytes 772
  51.2 1.4 %copy-start = (bf16[64,2,2048]{2,1,0:T(2,128)(2,1)S(1)}, bf16[64,2,2048]{2,1,0:T(2,128)(2,1)}, u32[]{:S(2)}) copy-start(bf16[64,2,2048]{2,1,0:T(2,128)(2,1)} %param.11) | copy-start | bytes 1572868

commit v2 on v1

--- a/solution.py
+++ b/solution.py
@@ -20,8 +20,9 @@
 MESH = pl.DeviceIdType.MESH
 
 
-def tail_kernel(
-    cfg, attended, incoming, gain, wo, wg, wu, wd, out,
+def layer_kernel(
+    cfg, holders, lengths, q, kv, place, incoming, gain, cache, wo, wg, wu, wd, out,
+    gq, gkv, of, tb, attended,
     wo_v, wg_v, wu_v, wd_v,
     fa, pa, oa, ra, res, h, ss, ssr,
     fg, s1, o1, r1, s2, o2, r2, hb,
@@ -31,8 +32,15 @@
     c1_ss, c1_rs, c2_ss, c2_rs,
     hp_ss, hp_rs, hx_ss, hx_rs, hf_ss, hf_rs,
     d_ss, d_rs,
+    cache_s, qp_ss, qp_rs, qx_ss, qx_rs, qf_ss, qf_rs,
+    tp_ss, tp_rs, tx_ss, tx_rs, tf_ss, tf_rs,
 ):
     Z, RB, T, NA, NF = cfg
+    S = cache.shape[0]
+    kv_local = cache.shape[2] // (2 * HD)
+    groups = H // KVH
+    QR = STEPS * groups
+    per = wd_v.shape[1] // CAP
     A = 4
     z = lax.axis_index("ffn")
     a = lax.axis_index("att")
@@ -46,13 +54,21 @@
             src.at[:, pl.ds(pl.multiple_of(k * T, T), T)], dst.at[k], sem.at[k]
         )
 
+    def kept_rows(i):
+        return pl.ds(pl.multiple_of((i % per) * CAP, CAP), CAP)
+
+    def cache_copy(i):
+        return pltpu.make_async_copy(cache.at[i], wd_v.at[i // per, kept_rows(i)], cache_s.at[i])
+
+    @pl.loop(0, S)
+    def _(i):
+        cache_copy(i).start()
+
     for k in range(NA):
         wcopy(wo, wo_v, wo_s, k).start()
     for k in range(NF):
         wcopy(wg, wg_v, wg_s, k).start()
         wcopy(wu, wu_v, wu_s, k).start()
-    for k in range(NA):
-        wcopy(wd, wd_v, wd_s, k).start()
 
     barrier = pltpu.get_barrier_semaphore()
     for d in range(1, Z):
@@ -101,6 +117,97 @@
     def d_copy(k, d):
         peer = (z + d) % Z
         return remote(pd.at[k, peer], rd.at[k, d - 1], d_ss.at[k, d - 1], d_rs.at[k, d - 1], "ffn", peer)
+
+    def block_of(ref, owner):
+        return ref.at[pl.ds(owner * S, S)]
+
+    for i, (mine, everyone) in enumerate(((q, gq), (kv, gkv))):
+        remote(mine, block_of(everyone, a), qx_ss.at[i], qx_rs.at[i], "att", xpeer).start()
+        remote(mine, block_of(everyone, a), qp_ss.at[i], qp_rs.at[i], "att", partner).start()
+        everyone[pl.ds(a * S, S)] = mine[...]
+
+    def qf_copy(i, everyone):
+        block = block_of(everyone, xpeer)
+        return remote(block, block, qf_ss.at[i], qf_rs.at[i], "att", partner)
+
+    far = 2 * (1 - x) + (1 - c)
+    for i, (mine, everyone) in enumerate(((q, gq), (kv, gkv))):
+        remote(mine, block_of(everyone, xpeer), qx_ss.at[i], qx_rs.at[i], "att", xpeer).wait_recv()
+        qf_copy(i, everyone).start()
+    for i, (mine, everyone) in enumerate(((q, gq), (kv, gkv))):
+        remote(mine, block_of(everyone, partner), qp_ss.at[i], qp_rs.at[i], "att", partner).wait_recv()
+        block = block_of(everyone, far)
+        remote(block, block, qf_ss.at[i], qf_rs.at[i], "att", partner).wait_recv()
+
+    def attend(i, g):
+        holder, length = holders[i], lengths[i]
+        rows = gq[holder][g * QR:(g + 1) * QR]
+        fresh = gkv[holder].astype(f32)
+        kept = kept_rows(i)
+        keys = wd_v[i // per, kept, g * 2 * HD:(g * 2 + 1) * HD]
+        values = wd_v[i // per, kept, (g * 2 + 1) * HD:(g * 2 + 2) * HD]
+        scale = HD ** (-0.5)
+        scores = lax.dot_general(
+            rows, keys, (((1,), (1,)), ((), ())), preferred_element_type=f32
+        ) * scale
+        column = lax.broadcasted_iota(jnp.int32, scores.shape, 1)
+        scores = jnp.where(column < length, scores, -jnp.inf)
+        wide = rows.astype(f32)
+        step = lax.broadcasted_iota(jnp.int32, (QR, 1), 0) // groups
+        new_scores = []
+        for t in range(STEPS):
+            at = g * 2 * STEPS + t
+            score = jnp.sum(wide * fresh[at:at + 1], -1, keepdims=True) * scale
+            new_scores.append(jnp.where(step >= t, score, -jnp.inf))
+        top = jnp.max(scores, -1, keepdims=True)
+        for score in new_scores:
+            top = jnp.maximum(top, score)
+        weights = jnp.exp(scores - top)
+        total = jnp.sum(weights, -1, keepdims=True)
+        new_weights = [jnp.exp(score - top) for score in new_scores]
+        for weight in new_weights:
+            total = total + weight
+        mixed = jnp.dot((weights / total).astype(bf), values, preferred_element_type=f32)
+        for t in range(STEPS):
+            at = g * 2 * STEPS + STEPS + t
+            mixed = mixed + (new_weights[t] / total).astype(bf).astype(f32) * fresh[at:at + 1]
+        of[pl.ds(pl.multiple_of(i * QR, QR), QR), :] = mixed
+
+    def t_copy(k, ss_, rs_, block, peer):
+        return remote(tb.at[k, block], tb.at[k, block], ss_.at[k], rs_.at[k], "att", peer)
+
+    heads = T // HD
+    chunks = groups // heads
+    for g in range(kv_local):
+        @pl.loop(0, S // 4)
+        def _(j):
+            for n in range(4):
+                if g == 0:
+                    cache_copy(j * 4 + n).wait()
+            for n in range(4):
+                attend(j * 4 + n, g)
+
+        for k in range(chunks):
+            for t in range(STEPS):
+                for n in range(heads):
+                    row = t * groups + k * heads + n
+                    tb[g * chunks + k, a, t * S:(t + 1) * S, n * HD:(n + 1) * HD] = of[
+                        pl.ds(row, S, stride=QR), :
+                    ].astype(bf)
+            t_copy(g * chunks + k, tx_ss, tx_rs, a, xpeer).start()
+            t_copy(g * chunks + k, tp_ss, tp_rs, a, partner).start()
+
+    for k in range(NA):
+        wcopy(wd, wd_v, wd_s, k).start()
+    for k in range(NA):
+        t_copy(k, tx_ss, tx_rs, xpeer, xpeer).wait_recv()
+        t_copy(k, tf_ss, tf_rs, xpeer, partner).start()
+    for k in range(NA):
+        t_copy(k, tp_ss, tp_rs, partner, partner).wait_recv()
+        t_copy(k, tf_ss, tf_rs, far, partner).wait_recv()
+        attended[:, k * T:(k + 1) * T] = jnp.dot(
+            place[...], tb[k].reshape(Z * RB, T), preferred_element_type=f32
+        ).astype(bf)
 
     @pl.loop(0, NA)
     def _(k):
@@ -113,7 +220,7 @@
             a_copy(k, d).start()
 
     for k in range(NA):
-        total = incoming[z, :, k * T:(k + 1) * T].astype(f32) + oa[k]
+        total = incoming[:, k * T:(k + 1) * T].astype(f32) + oa[k]
         for d in range(1, Z):
             a_copy(k, d).wait_recv()
             total = total + ra[k, d - 1].astype(f32)
@@ -215,6 +322,14 @@
             d_copy(k, d).wait_send()
     for d in range(1, A):
         q_copy(d).wait_send()
+    for i, (mine, everyone) in enumerate(((q, gq), (kv, gkv))):
+        remote(mine, block_of(everyone, a), qx_ss.at[i], qx_rs.at[i], "att", xpeer).wait_send()
+        remote(mine, block_of(everyone, a), qp_ss.at[i], qp_rs.at[i], "att", partner).wait_send()
+        qf_copy(i, everyone).wait_send()
+    for k in range(NA):
+        t_copy(k, tx_ss, tx_rs, a, xpeer).wait_send()
+        t_copy(k, tp_ss, tp_rs, a, partner).wait_send()
+        t_copy(k, tf_ss, tf_rs, xpeer, partner).wait_send()
     for k in range(NF):
         c1_copy(k).wait_send()
         c2_copy(k).wait_send()
@@ -223,20 +338,24 @@
         hf_copy(k, xpeer).wait_send()
 
 
-def tail(attended, incoming, gain, w_out, w_gate, w_up, w_down):
+def fused(holders, lengths, q, kv, place, incoming, gain, cache, w_out, w_gate, w_up, w_down):
     Z = lax.axis_size("ffn")
-    rows, kdim = attended.shape
+    rows, kdim = place.shape[0], w_out.shape[0]
     width = w_out.shape[1]
     units = w_gate.shape[1]
     RB, T = rows // Z, TILE
     NA, NF = width // T, units // T
     AB = rows // 4
+    S = cache.shape[0]
     bf, f32 = jnp.bfloat16, jnp.float32
     V = pltpu.VMEM
     dma = pltpu.SemaphoreType.DMA
     vm = pl.BlockSpec(memory_space=pltpu.VMEM)
+    sm = pl.BlockSpec(memory_space=pltpu.SMEM)
     hbm = pl.BlockSpec(memory_space=pl.ANY)
     scratch = [
+        V((4 * S,) + q.shape[1:], bf), V((4 * S,) + kv.shape[1:], bf),
+        V((S * STEPS * (H // KVH), HD), f32), V((kdim // T, 4, AB, T), bf), V((rows, kdim), bf),
         V((NA, kdim, T), bf), V((NF, width, T), bf), V((NF, width, T), bf), V((NA, units, T), bf),
         V((Z, RB, T), f32), V((NA, Z, RB, T), bf), V((NA, RB, T), f32), V((NA, Z - 1, RB, T), bf),
         V((NA, Z, RB, T), bf), V((rows, width), bf), V((4, AB, 128), f32), V((3, AB, 128), f32),
@@ -247,23 +366,79 @@
         dma((NA,)), dma((NF,)), dma((NF,)), dma((NA,)),
         dma((NA, Z - 1)), dma((NA, Z - 1)), dma((NA, Z - 1)), dma((NA, Z - 1)), dma((3,)), dma((3,)),
     ] + [dma((NF,)) for _ in range(10)] + [dma((NA, Z - 1)), dma((NA, Z - 1))]
+    scratch += [dma((S,))] + [dma((2,)) for _ in range(6)] + [dma((NA,)) for _ in range(6)]
     return pl.pallas_call(
-        functools.partial(tail_kernel, (Z, RB, T, NA, NF)),
+        functools.partial(layer_kernel, (Z, RB, T, NA, NF)),
         out_shape=jax.ShapeDtypeStruct((RB, width), bf),
-        in_specs=[vm, vm, vm, hbm, hbm, hbm, hbm],
+        in_specs=[sm, sm, vm, vm, vm, vm, vm, hbm, hbm, hbm, hbm, hbm],
         out_specs=vm,
         scratch_shapes=scratch,
         compiler_params=pltpu.CompilerParams(
             collective_id=1, has_side_effects=True, vmem_limit_bytes=67043328
         ),
-    )(attended, incoming, gain, w_out, w_gate, w_up, w_down)
+    )(holders, lengths, q, kv, place, incoming, gain, cache, w_out, w_gate, w_up, w_down)
+
+
+def fits(queries, cache, w_out, w_gate, slot_of):
+    slots = cache.shape[0]
+    chunks = w_out.shape[1] // TILE
+    return (
+        lax.axis_size("att") == 4
+        and lax.axis_size("ffn") == 4
+        and slots % 16 == 0
+        and slot_of.shape[0] == 4 * slots
+        and slot_of.shape[0] * STEPS <= 128
+        and cache.shape[2] == TILE
+        and w_out.shape == (chunks * TILE, chunks * TILE)
+        and w_gate.shape[1] % TILE == 0
+        and chunks * (w_gate.shape[1] // CAP) >= slots
+    )
+
+
+def local_fused(
+    incoming, queries, new_kv, cache, lengths, slot_of, w_out, norm_gain, w_gate, w_up, w_down
+):
+    slots, requests = cache.shape[0], slot_of.shape[0]
+    kv_local, groups = cache.shape[2] // (2 * HD), H // KVH
+    width = incoming.shape[2]
+    own_rows = requests // lax.axis_size("ffn")
+    own_slots = lax.axis_index("att") * slots + jnp.arange(slots, dtype=jnp.int32)
+    held = slot_of[None, :] == own_slots[:, None]
+    holders = jnp.sum(jnp.where(held, jnp.arange(requests, dtype=jnp.int32)[None, :], 0), 1)
+    q = queries.reshape(slots, STEPS, kv_local, groups, HD).transpose(0, 2, 1, 3, 4)
+    kv = new_kv.reshape(slots, STEPS, kv_local, 2, HD).transpose(0, 2, 3, 1, 4)
+    gathered_row = (slot_of // slots) * (slots * STEPS) + slot_of % slots
+    gathered_row = gathered_row[:, None] + slots * jnp.arange(STEPS, dtype=jnp.int32)[None, :]
+    place = (
+        gathered_row.reshape(-1, 1) == jnp.arange(requests * STEPS, dtype=jnp.int32)[None, :]
+    ).astype(jnp.bfloat16)
+    mine = lax.dynamic_slice_in_dim(incoming, lax.axis_index("ffn") * own_rows, own_rows)
+    own = fused(
+        holders,
+        lengths,
+        q.reshape(slots, -1, HD),
+        kv.reshape(slots, -1, HD),
+        place,
+        mine.reshape(own_rows * STEPS, width),
+        norm_gain[None],
+        cache,
+        w_out,
+        w_gate,
+        w_up,
+        w_down,
+    )
+    return own.reshape(own_rows, STEPS, width)
 
 
 def local(
     incoming, queries, new_kv, cache, lengths, slot_of, w_out, norm_gain, w_gate, w_up, w_down
 ):
+    if fits(queries, cache, w_out, w_gate, slot_of):
+        return local_fused(
+            incoming, queries, new_kv, cache, lengths, slot_of,
+            w_out, norm_gain, w_gate, w_up, w_down,
+        )
     ffn_count = lax.axis_size("ffn")
-    fast = lax.axis_size("att") == 4 and slot_of.shape[0] * STEPS <= 128
     att_index = lax.axis_index("att")
     ffn_index = lax.axis_index("ffn")
     request_count = slot_of.shape[0]
@@ -326,17 +501,6 @@
     shard_rows = lax.all_gather(attended, "att", axis=0, tiled=True)
     row_count = shard_rows.shape[0]
     flattened = shard_rows.reshape(row_count * STEPS, shard_rows.shape[2])
-    if fast:
-        own = tail(
-            jnp.take(shard_rows, slot_of, axis=0).reshape(row_count * STEPS, -1),
-            incoming.reshape(ffn_count, -1, incoming.shape[2]),
-            norm_gain[None],
-            w_out,
-            w_gate,
-            w_up,
-            w_down,
-        )
-        return own.reshape(-1, STEPS, incoming.shape[2])
     heads_slots = jnp.dot(flattened, w_out, preferred_element_type=jnp.float32).reshape(
         row_count, STEPS, w_out.shape[1]
     )

time: 125 us -> 98.6 us (0.79)
  blocking collectives: 21.8 us -> 0 us
  Pallas kernels: 68.7 us -> 90.4 us
  local copies, waits for them, and re-layouts: 21.9 us -> 5.15 us
  matrix products: 8.92 us -> 0 us
    all_gather x3 -> x0, blocking collectives: 21.8 us -> none  [the longest x1 7.77 us: local(): lax.all_gather(queries, 'att', axis=0, tiled=True)]
    pallas_call x1, Pallas kernels: 68.7 us -> 90.4 us  [fused(): pl.pallas_call(functools.partial(layer_kernel, (Z, RB, T, NA, NF)), out_s...]
    unnamed x7 -> x0, local copies, waits for them, and re-layouts: 14.8 us -> none
    dot_general x4 -> x0, matrix products: 8.92 us -> none  [the longest x1 4.26 us: local(): jnp.einsum('rskgc,rckd->rskgd', kept_prob, cache_view[:, :, :, 1], prefer...]
    gather x6 -> x0, local copies, waits for them, and re-layouts: 3.36 us -> none  [the longest x2 1.8 us: local(): jnp.take(shard_rows, slot_of, axis=0).reshape(row_count * STEPS, -1)]
    select_n x3 -> x0, other arithmetic: 1.67 us -> none  [the longest x2 1.57 us: local(): jnp.take(shard_rows, slot_of, axis=0).reshape(row_count * STEPS, -1)]
    reshape x4, local copies, waits for them, and re-layouts: 2.73 us -> 4.02 us  [the longest x2 1.66 us: local_fused(): queries.reshape(slots, STEPS, kv_local, groups, HD).transpose(0, 2, 1, 3, 4)]
where the time goes in v2:
time: 98.6 us; the launch traced here: 98.4 us
  Pallas kernels  90.4 us (92%)
  local copies, waits for them, and re-layouts  5.15 us (5%)
  other arithmetic  2.76 us (3%)
    pallas_call x1, Pallas kernels, fused(): pl.pallas_call(functools.partial(layer_kernel, (Z, RB, T, NA, NF)), out_s...  90.4 us

profile of v2, /device:TPU:0, one launch (start us, length us, event | category | flops | bytes accessed | tf_op | source)
XLA Modules:
  0.0 98.4 jit_solution(4512504255031175467)
XLA Ops:
  0.0 1.3 %select_reduce_fusion.holders = s32[16]{0:T(128)} fusion(s32[64]{0:T(128)} %param.16, s32[16]{0:T(128)S(1)} %iota_add_fusion), kind=kLoop, calls=%fused_computation.3 | loop fusion | flops 3056 | bytes 384 | tf_op jit(solution)/shard_map/reduce_sum | solution.py:407
  1.3 0.7 fusion.1
  2.0 0.1 broadcast_add_fusion
  2.1 0.1 add.50
  2.2 0.7 fusion.place
  2.9 1.0 %constant_dynamic-slice_fusion = bf16[16,2,2048]{2,1,0:T(2,128)(2,1)S(1)} fusion(bf16[64,2,2048]{2,1,0:T(2,128)(2,1)} %param.11, s32[]{:T(128)S(6)} %select_n.22), kind=kLoop, calls=%fused_computation.12 | loop fusion | bytes 262148 | tf_op jit(solution)/shard_map/dynamic_slice | solution.py:415
  3.9 0.7 reshape.48.incoming
  4.6 1.0 %reshape.44 = bf16[16,2,2,8,128]{4,3,2,1,0:T(8,128)(2,1)S(1)} reshape(bf16[16,2,2048]{2,1,0:T(2,128)(2,1)} %param.12) | data formatting | bytes 262144 | tf_op jit(solution)/shard_map/reshape | solution.py:408
  5.6 0.7 copy.16
  6.3 90.4 %shard_map.109 = bf16[32,2048]{1,0:T(8,128)(2,1)} custom-call(s32[16]{0:T(128)} %select_reduce_fusion.holders, s32[16]{0:T(128)} %lengths.1, bf16[16,32,128]{2,1,0:T(8,128)(2,1)} %bitcast.9, bf16[16,8,128]{2,1,0:T(8,128)(2,1)} %bitcast.10, bf16[128,128]{1,0:T(8,128)(2,1)} %fusion.place, bf16[32,2048]{1,0:T(8,128)(2,1)} %reshape.48.incoming, ...), custom_call_target="tpu_custom_call" | custom-call | tf_op jit(solution)/shard_map/pallas_call | solution.py:370
  96.7 1.7 %reshape.49 = bf16[16,2,2048]{2,1,0:T(2,128)(2,1)} reshape(bf16[32,2048]{1,0:T(8,128)(2,1)} %shard_map.109) | data formatting | bytes 262144 | tf_op jit(solution)/shard_map/reshape | solution.py:430
  (2 shorter events, 0.0 us)

commit v3 on v2

--- a/solution.py
+++ b/solution.py
@@ -21,14 +21,14 @@
 
 
 def layer_kernel(
-    cfg, holders, lengths, q, kv, place, incoming, gain, cache, wo, wg, wu, wd, out,
-    gq, gkv, of, tb, attended,
+    cfg, holders, slots_row, lengths, q, kv, incoming, gain, cache, wo, wg, wu, wd, out,
+    place, kept_in, gq, gkv, of, tb, attended,
     wo_v, wg_v, wu_v, wd_v,
-    fa, pa, oa, ra, res, h, ss, ssr,
+    fa, pa, ra, sm, rm, om, res, h, ss, ssr,
     fg, s1, o1, r1, s2, o2, r2, hb,
     pd, od, rd,
     wo_s, wg_s, wu_s, wd_s,
-    a_ss, a_rs, b_ss, b_rs, q_ss, q_rs,
+    in_s, a_ss, a_rs, m_ss, m_rs, g_ss, g_rs, n_ss, n_rs, f_ss, f_rs, q_ss, q_rs,
     c1_ss, c1_rs, c2_ss, c2_rs,
     hp_ss, hp_rs, hx_ss, hx_rs, hf_ss, hf_rs,
     d_ss, d_rs,
@@ -64,6 +64,11 @@
     def _(i):
         cache_copy(i).start()
 
+    half = z // 2
+    in_copy = pltpu.make_async_copy(
+        incoming.at[pl.ds(half * kept_in.shape[0], kept_in.shape[0])], kept_in, in_s.at[0]
+    )
+    in_copy.start()
     for k in range(NA):
         wcopy(wo, wo_v, wo_s, k).start()
     for k in range(NF):
@@ -83,17 +88,31 @@
             device_id={axis: peer}, device_id_type=MESH,
         )
 
-    def a_copy(k, d):
-        peer = (z + d) % Z
-        return remote(pa.at[k, peer], ra.at[k, d - 1], a_ss.at[k, d - 1], a_rs.at[k, d - 1], "ffn", peer)
-
-    def b_copy(k, d):
-        peer = (z + d) % Z
-        return remote(res.at[k, z], res.at[k, z], b_ss.at[k, d - 1], b_rs.at[k, d - 1], "ffn", peer)
-
-    def b_wait(k, d):
-        origin = (z + Z - d) % Z
-        remote(res.at[k, origin], res.at[k, origin], b_ss.at[k, d - 1], b_rs.at[k, d - 1], "ffn", origin).wait_recv()
+    inside = z * (Z - 1 - z)
+    inner = 1 + half
+    outer = 3 * (z - 1)
+    other = 3 - z
+
+    def half_of(ref, k, which):
+        return ref.at[k, which]
+
+    def a_copy(k, peer):
+        return remote(pa.at[k], ra.at[k], a_ss.at[k], a_rs.at[k], "ffn", peer)
+
+    def m_copy(k):
+        return remote(sm.at[k], rm.at[k], m_ss.at[k], m_rs.at[k], "ffn", other)
+
+    def g_copy(k, which):
+        block = half_of(res, k, which)
+        return remote(block, block, g_ss.at[k], g_rs.at[k], "ffn", other)
+
+    def n_copy(k, which, peer):
+        block = half_of(res, k, which)
+        return remote(block, block, n_ss.at[k], n_rs.at[k], "ffn", peer)
+
+    def f_copy(k, which, peer):
+        block = half_of(res, k, which)
+        return remote(block, block, f_ss.at[k], f_rs.at[k], "ffn", peer)
 
     def q_copy(d):
         peer = (a + d) % A
@@ -129,6 +148,24 @@
     def qf_copy(i, everyone):
         block = block_of(everyone, xpeer)
         return remote(block, block, qf_ss.at[i], qf_rs.at[i], "att", partner)
+
+    R = slots_row.shape[1]
+
+    shift = S.bit_length() - 1
+    spread_row = lax.broadcasted_iota(jnp.int32, (R, R * STEPS), 0) * STEPS
+    spread_col = lax.broadcasted_iota(jnp.int32, (R, R * STEPS), 1)
+    spread = (spread_col >= spread_row) & (spread_col < spread_row + STEPS)
+    slot_at = jnp.dot(
+        jnp.broadcast_to(slots_row[...].astype(f32), (8, R)).astype(bf),
+        jnp.where(spread, 1.0, 0.0).astype(bf),
+        preferred_element_type=f32,
+    )[:1]
+    row = lax.broadcasted_iota(jnp.int32, (R * STEPS, R * STEPS), 0)
+    col = lax.broadcasted_iota(jnp.int32, (R * STEPS, R * STEPS), 1)
+    row_slot = ((row >> (shift + 1)) << shift) + (row & (S - 1))
+    row_step = (row >> shift) & (STEPS - 1)
+    chosen = (row_slot.astype(f32) == slot_at) & (row_step == (col & (STEPS - 1)))
+    place[...] = jnp.where(chosen, 1.0, 0.0).astype(bf)
 
     far = 2 * (1 - x) + (1 - c)
     for i, (mine, everyone) in enumerate(((q, gq), (kv, gkv))):
@@ -205,34 +242,59 @@
     for k in range(NA):
         t_copy(k, tp_ss, tp_rs, partner, partner).wait_recv()
         t_copy(k, tf_ss, tf_rs, far, partner).wait_recv()
-        attended[:, k * T:(k + 1) * T] = jnp.dot(
-            place[...], tb[k].reshape(Z * RB, T), preferred_element_type=f32
+        attended[:, k * T:(k + 1) * T] = lax.dot_general(
+            place[...], tb[k].reshape(Z * RB, T), (((0,), (0,)), ((), ())),
+            preferred_element_type=f32,
         ).astype(bf)
 
-    @pl.loop(0, NA)
-    def _(k):
+    in_copy.wait()
+
+    def own_half(k):
+        m_copy(k).wait_recv()
+        kept = kept_in[:, :, k * T:(k + 1) * T].astype(f32).reshape(2, RB, T)
+        res[k, half] = (kept + om[k] + rm[k].astype(f32)).astype(bf)
+        g_copy(k, half).start()
+        n_copy(k, half, outer).start()
+
+    def pass_on(k):
+        g_copy(k, 1 - half).wait_recv()
+        f_copy(k, 1 - half, outer).start()
+
+    for k in range(NA):
         wcopy(wo, wo_v, wo_s, k).wait()
-        p = jnp.dot(attended[...], wo_v[k], preferred_element_type=f32).reshape(Z, RB, T)
-        fa[...] = p
-        pa[k] = p.astype(bf)
-        oa[k] = fa[z]
-        for d in range(1, Z):
-            a_copy(k, d).start()
-
-    for k in range(NA):
-        total = incoming[:, k * T:(k + 1) * T].astype(f32) + oa[k]
-        for d in range(1, Z):
-            a_copy(k, d).wait_recv()
-            total = total + ra[k, d - 1].astype(f32)
-        res[k, z] = total.astype(bf)
-        for d in range(1, Z):
-            b_copy(k, d).start()
+        fa[...] = jnp.dot(attended[...], wo_v[k], preferred_element_type=f32).reshape(fa.shape)
+
+        @pl.when(inside == 0)
+        def _():
+            pa[k] = fa[...].astype(bf)
+            a_copy(k, inner).start()
+
+        @pl.when(inside > 0)
+        def _():
+            a_copy(k, outer).wait_recv()
+            theirs = 1 - half
+            sm[k] = (fa[theirs] + ra[k, theirs].astype(f32)).astype(bf)
+            m_copy(k).start()
+            om[k] = fa[half] + ra[k, half].astype(f32)
+            if k > 0:
+                own_half(k - 1)
+            if k > 1:
+                pass_on(k - 2)
+
+    @pl.when(inside > 0)
+    def _():
+        own_half(NA - 1)
+        for k in range(max(NA - 2, 0), NA):
+            pass_on(k)
 
     squares = jnp.zeros((Z, RB, 1), f32)
     for k in range(NA):
-        for d in range(1, Z):
-            b_wait(k, d)
-        wide = res[k].astype(f32)
+        @pl.when(inside == 0)
+        def _():
+            n_copy(k, half, inner).wait_recv()
+            f_copy(k, 1 - half, inner).wait_recv()
+
+        wide = res[k].astype(f32).reshape(Z, RB, T)
         squares = squares + jnp.sum(wide * wide, -1, keepdims=True)
         h[:, k * T:(k + 1) * T] = (
             (wide * gain[:, k * T:(k + 1) * T]).astype(bf).reshape(Z * RB, T)
@@ -249,14 +311,14 @@
             fg[i] = p.reshape(fg.shape[1:])
             for xx in range(2):
                 s1[k, i, xx] = fg[i, 2 * xx + (1 - c)].astype(bf)
-                o1[k, i, xx] = fg[i, 2 * xx + c]
+                o1[k % 2, i, xx] = fg[i, 2 * xx + c]
         c1_copy(k).start()
 
     def second(k):
         c1_copy(k).wait_recv()
         for i in range(2):
-            s2[k, i] = (o1[k, i, 1 - x] + r1[k, i, 1 - x].astype(f32)).astype(bf)
-            o2[k, i] = o1[k, i, x] + r1[k, i, x].astype(f32)
+            s2[k, i] = (o1[k % 2, i, 1 - x] + r1[k, i, 1 - x].astype(f32)).astype(bf)
+            o2[k, i] = o1[k % 2, i, x] + r1[k, i, x].astype(f32)
         c2_copy(k).start()
 
     first(0)
@@ -302,24 +364,36 @@
                 hb[k].reshape(Z * RB, T), wd_v[n, k * T:(k + 1) * T, :], preferred_element_type=f32
             )
         p = p.reshape(Z, RB, T)
-        fa[...] = p
+        fa[...] = p.reshape(fa.shape)
         pd[n] = p.astype(bf)
-        od[n] = fa[z]
+        od[n] = fa[half, z % 2]
         for d in range(1, Z):
             d_copy(n, d).start()
 
     for n in range(NA):
-        total = res[n, z].astype(f32) + od[n]
+        total = res[n, half, z % 2].astype(f32) + od[n]
         for d in range(1, Z):
             d_copy(n, d).wait_recv()
             total = total + rd[n, d - 1].astype(f32)
-        out[:, n * T:(n + 1) * T] = total.astype(bf)
+        out[:, :, n * T:(n + 1) * T] = total.reshape(out.shape[0], STEPS, T).astype(bf)
 
     for k in range(NA):
         for d in range(1, Z):
-            a_copy(k, d).wait_send()
-            b_copy(k, d).wait_send()
             d_copy(k, d).wait_send()
+
+    @pl.when(inside == 0)
+    def _():
+        for k in range(NA):
+            a_copy(k, inner).wait_send()
+
+    @pl.when(inside > 0)
+    def _():
+        for k in range(NA):
+            m_copy(k).wait_send()
+            g_copy(k, half).wait_send()
+            n_copy(k, half, outer).wait_send()
+            f_copy(k, 1 - half, outer).wait_send()
+
     for d in range(1, A):
         q_copy(d).wait_send()
     for i, (mine, everyone) in enumerate(((q, gq), (kv, gkv))):
@@ -338,9 +412,9 @@
         hf_copy(k, xpeer).wait_send()
 
 
-def fused(holders, lengths, q, kv, place, incoming, gain, cache, w_out, w_gate, w_up, w_down):
+def fused(holders, slots, lengths, q, kv, incoming, gain, cache, w_out, w_gate, w_up, w_down):
     Z = lax.axis_size("ffn")
-    rows, kdim = place.shape[0], w_out.shape[0]
+    rows, kdim = slots.shape[0] * STEPS, w_out.shape[0]
     width = w_out.shape[1]
     units = w_gate.shape[1]
     RB, T = rows // Z, TILE
@@ -354,29 +428,32 @@
     sm = pl.BlockSpec(memory_space=pltpu.SMEM)
     hbm = pl.BlockSpec(memory_space=pl.ANY)
     scratch = [
+        V((rows, rows), bf), V((incoming.shape[0] // 2,) + incoming.shape[1:], bf),
         V((4 * S,) + q.shape[1:], bf), V((4 * S,) + kv.shape[1:], bf),
         V((S * STEPS * (H // KVH), HD), f32), V((kdim // T, 4, AB, T), bf), V((rows, kdim), bf),
         V((NA, kdim, T), bf), V((NF, width, T), bf), V((NF, width, T), bf), V((NA, units, T), bf),
-        V((Z, RB, T), f32), V((NA, Z, RB, T), bf), V((NA, RB, T), f32), V((NA, Z - 1, RB, T), bf),
-        V((NA, Z, RB, T), bf), V((rows, width), bf), V((4, AB, 128), f32), V((3, AB, 128), f32),
-        V((2, 4, AB, T), f32), V((NF, 2, 2, AB, T), bf), V((NF, 2, 2, AB, T), f32),
+        V((2, 2, RB, T), f32), V((NA, 2, 2, RB, T), bf), V((NA, 2, 2, RB, T), bf), V((NA, 2, RB, T), bf),
+        V((NA, 2, RB, T), bf), V((NA, 2, RB, T), f32),
+        V((NA, 2, 2, RB, T), bf), V((rows, width), bf), V((4, AB, 128), f32), V((3, AB, 128), f32),
+        V((2, 4, AB, T), f32), V((NF, 2, 2, AB, T), bf), V((2, 2, 2, AB, T), f32),
         V((NF, 2, 2, AB, T), bf), V((NF, 2, AB, T), bf), V((NF, 2, AB, T), f32),
         V((NF, 2, AB, T), bf), V((NF, 4, AB, T), bf),
         V((NA, Z, RB, T), bf), V((NA, RB, T), f32), V((NA, Z - 1, RB, T), bf),
         dma((NA,)), dma((NF,)), dma((NF,)), dma((NA,)),
-        dma((NA, Z - 1)), dma((NA, Z - 1)), dma((NA, Z - 1)), dma((NA, Z - 1)), dma((3,)), dma((3,)),
-    ] + [dma((NF,)) for _ in range(10)] + [dma((NA, Z - 1)), dma((NA, Z - 1))]
+        dma((1,)),
+    ] + [dma((NA,)) for _ in range(10)] + [dma((3,)), dma((3,))]
+    scratch += [dma((NF,)) for _ in range(10)] + [dma((NA, Z - 1)), dma((NA, Z - 1))]
     scratch += [dma((S,))] + [dma((2,)) for _ in range(6)] + [dma((NA,)) for _ in range(6)]
     return pl.pallas_call(
         functools.partial(layer_kernel, (Z, RB, T, NA, NF)),
-        out_shape=jax.ShapeDtypeStruct((RB, width), bf),
-        in_specs=[sm, sm, vm, vm, vm, vm, vm, hbm, hbm, hbm, hbm, hbm],
+        out_shape=jax.ShapeDtypeStruct((RB // STEPS, STEPS, width), bf),
+        in_specs=[sm, vm, sm, vm, vm, hbm, vm, hbm, hbm, hbm, hbm, hbm],
         out_specs=vm,
         scratch_shapes=scratch,
         compiler_params=pltpu.CompilerParams(
             collective_id=1, has_side_effects=True, vmem_limit_bytes=67043328
         ),
-    )(holders, lengths, q, kv, place, incoming, gain, cache, w_out, w_gate, w_up, w_down)
+    )(holders, slots[None], lengths, q, kv, incoming, gain, cache, w_out, w_gate, w_up, w_down)
 
 
 def fits(queries, cache, w_out, w_gate, slot_of):
@@ -386,6 +463,7 @@
         lax.axis_size("att") == 4
         and lax.axis_size("ffn") == 4
         and slots % 16 == 0
+        and slots & (slots - 1) == 0
         and slot_of.shape[0] == 4 * slots
         and slot_of.shape[0] * STEPS <= 128
         and cache.shape[2] == TILE
@@ -398,28 +476,20 @@
 def local_fused(
     incoming, queries, new_kv, cache, lengths, slot_of, w_out, norm_gain, w_gate, w_up, w_down
 ):
-    slots, requests = cache.shape[0], slot_of.shape[0]
+    slots = cache.shape[0]
     kv_local, groups = cache.shape[2] // (2 * HD), H // KVH
-    width = incoming.shape[2]
-    own_rows = requests // lax.axis_size("ffn")
+    q = queries.reshape(slots, STEPS, kv_local, groups, HD).transpose(0, 2, 1, 3, 4)
+    kv = new_kv.reshape(slots, STEPS, kv_local, 2, HD).transpose(0, 2, 3, 1, 4)
+    requests = jnp.arange(slot_of.shape[0], dtype=jnp.int32)
     own_slots = lax.axis_index("att") * slots + jnp.arange(slots, dtype=jnp.int32)
     held = slot_of[None, :] == own_slots[:, None]
-    holders = jnp.sum(jnp.where(held, jnp.arange(requests, dtype=jnp.int32)[None, :], 0), 1)
-    q = queries.reshape(slots, STEPS, kv_local, groups, HD).transpose(0, 2, 1, 3, 4)
-    kv = new_kv.reshape(slots, STEPS, kv_local, 2, HD).transpose(0, 2, 3, 1, 4)
-    gathered_row = (slot_of // slots) * (slots * STEPS) + slot_of % slots
-    gathered_row = gathered_row[:, None] + slots * jnp.arange(STEPS, dtype=jnp.int32)[None, :]
-    place = (
-        gathered_row.reshape(-1, 1) == jnp.arange(requests * STEPS, dtype=jnp.int32)[None, :]
-    ).astype(jnp.bfloat16)
-    mine = lax.dynamic_slice_in_dim(incoming, lax.axis_index("ffn") * own_rows, own_rows)
-    own = fused(
-        holders,
+    return fused(
+        jnp.sum(jnp.where(held, requests[None, :], 0), 1),
+        slot_of,
         lengths,
         q.reshape(slots, -1, HD),
         kv.reshape(slots, -1, HD),
-        place,
-        mine.reshape(own_rows * STEPS, width),
+        incoming,
         norm_gain[None],
         cache,
         w_out,
@@ -427,7 +497,6 @@
         w_up,
         w_down,
     )
-    return own.reshape(own_rows, STEPS, width)
 
 
 def local(

time: 98.6 us -> 91.9 us (0.932)
  Pallas kernels: 90.4 us -> 87 us
  local copies, waits for them, and re-layouts: 5.15 us -> 3.32 us
  other arithmetic: 2.76 us -> 1.34 us
    pallas_call x1, Pallas kernels: 90.4 us -> 87 us  [fused(): pl.pallas_call(functools.partial(layer_kernel, (Z, RB, T, NA, NF)), out_s...]
    reshape x2 -> x0, local copies, waits for them, and re-layouts: 2.35 us -> none  [the longest x1 1.66 us: local_fused(): return own.reshape(own_rows, STEPS, width)]
    unnamed x0 -> x1, local copies, waits for them, and re-layouts: none -> 1.65 us
    dynamic_slice x1 -> x0, local copies, waits for them, and re-layouts: 1 us -> none  [local_fused(): lax.dynamic_slice_in_dim(incoming, lax.axis_index('ffn') * own_rows, own_...]
where the time goes in v3:
time: 91.9 us; the launch traced here: 91.7 us
  Pallas kernels  87 us (95%)
  local copies, waits for them, and re-layouts  3.32 us (4%)
  other arithmetic  1.34 us (1%)
    pallas_call x1, Pallas kernels, fused(): pl.pallas_call(functools.partial(layer_kernel, (Z, RB, T, NA, NF)), out_s...  87 us

profile of v3, /device:TPU:0, one launch (start us, length us, event | category | flops | bytes accessed | tf_op | source)
XLA Modules:
  0.0 91.7 jit_solution(10953358442812735152)
XLA Ops:
  0.0 1.3 %select_reduce_fusion.holders = s32[16]{0:T(128)} fusion(s32[64]{0:T(128)} %param.16, s32[16]{0:T(128)S(1)} %iota_add_fusion), kind=kLoop, calls=%fused_computation | loop fusion | flops 3056 | bytes 384 | tf_op jit(solution)/shard_map/reduce_sum | solution.py:487
  1.3 1.0 %reshape.17 = bf16[16,2,2,8,128]{4,3,2,1,0:T(8,128)(2,1)S(1)} reshape(bf16[16,2,2048]{2,1,0:T(2,128)(2,1)} %param.12) | data formatting | bytes 262144 | tf_op jit(solution)/shard_map/reshape | solution.py:481
  2.3 0.7 copy.14
  3.0 87.0 %shard_map.109 = bf16[16,2,2048]{2,1,0:T(2,128)(2,1)} custom-call(s32[16]{0:T(128)} %select_reduce_fusion.holders, s32[1,64]{1,0:T(1,128)} %bitcast.13, s32[16]{0:T(128)} %lengths.1, bf16[16,32,128]{2,1,0:T(8,128)(2,1)} %bitcast.10, bf16[16,8,128]{2,1,0:T(8,128)(2,1)} %bitcast.11, bf16[64,2,2048]{2,1,0:T(2,128)(2,1)} %incoming.1, f32[1,2048]{1,0:T(1,128)} %bitcast.12, ...), custom_call_target="tpu_custom_call" | custom-call | tf_op jit(solution)/shard_map/pallas_call | solution.py:447
  90.0 1.7 %copy.17 = bf16[16,2,2048]{2,1,0:T(2,128)(2,1)} copy(bf16[16,2,2048]{2,1,0:T(2,128)(2,1)} %shard_map.109) | data formatting | bytes 262144
  (1 shorter events, 0.0 us)

commit v4 on v3

--- a/solution.py
+++ b/solution.py
@@ -17,6 +17,7 @@
 
 epsilon = 1e-05
 TILE = 512
+LAG = 3
 MESH = pl.DeviceIdType.MESH
 
 
@@ -321,29 +322,38 @@
             o2[k, i] = o1[k % 2, i, x] + r1[k, i, x].astype(f32)
         c2_copy(k).start()
 
-    first(0)
-
-    @pl.loop(1, NF)
-    def _(k):
-        first(k)
-        second(k - 1)
-
-    second(NF - 1)
-
-    total_squares = ss[a]
-    for d in range(1, A):
-        q_copy(d).wait_recv()
-        total_squares = total_squares + ssr[d - 1]
-    inverse = lax.rsqrt(total_squares / D + epsilon)[:, :1]
-
-    @pl.loop(0, NF)
-    def _(k):
+    def hidden(k, inverse):
         c2_copy(k).wait_recv()
         gate = (o2[k, 0] + r2[k, 0].astype(f32)) * inverse
         up = (o2[k, 1] + r2[k, 1].astype(f32)) * inverse
         hb[k, a] = (gate / (1.0 + jnp.exp(-gate)) * up).astype(bf)
         hx_copy(k, a).start()
         hp_copy(k, a).start()
+
+    first(0)
+
+    @pl.loop(1, LAG)
+    def _(k):
+        first(k)
+        second(k - 1)
+
+    total_squares = ss[a]
+    for d in range(1, A):
+        q_copy(d).wait_recv()
+        total_squares = total_squares + ssr[d - 1]
+    inverse = lax.rsqrt(total_squares / D + epsilon)[:, :1]
+
+    @pl.loop(LAG, NF)
+    def _(k):
+        first(k)
+        second(k - 1)
+        hidden(k - LAG, inverse)
+
+    second(NF - 1)
+
+    @pl.loop(NF - LAG, NF)
+    def _(k):
+        hidden(k, inverse)
 
     @pl.loop(0, NF)
     def _(k):
@@ -469,6 +479,7 @@
         and cache.shape[2] == TILE
         and w_out.shape == (chunks * TILE, chunks * TILE)
         and w_gate.shape[1] % TILE == 0
+        and w_gate.shape[1] // TILE > LAG
         and chunks * (w_gate.shape[1] // CAP) >= slots
     )
 

time: 91.9 us -> 92.4 us (level)
  no operation moved by 1% of the time
where the time goes in v4:
time: 92.4 us; the launch traced here: 91.9 us
  Pallas kernels  87.2 us (94%)
  local copies, waits for them, and re-layouts  3.32 us (4%)
  other arithmetic  1.34 us (1%)
    pallas_call x1, Pallas kernels, fused(): pl.pallas_call(functools.partial(layer_kernel, (Z, RB, T, NA, NF)), out_s...  87.2 us

profile of v4, /device:TPU:0, one launch (start us, length us, event | category | flops | bytes accessed | tf_op | source)
XLA Modules:
  0.0 91.9 jit_solution(852131645851466455)
XLA Ops:
  0.0 1.3 %select_reduce_fusion.holders = s32[16]{0:T(128)} fusion(s32[64]{0:T(128)} %param.16, s32[16]{0:T(128)S(1)} %iota_add_fusion), kind=kLoop, calls=%fused_computation | loop fusion | flops 3056 | bytes 384 | tf_op jit(solution)/shard_map/reduce_sum | solution.py:498
  1.3 1.0 %reshape.17 = bf16[16,2,2,8,128]{4,3,2,1,0:T(8,128)(2,1)S(1)} reshape(bf16[16,2,2048]{2,1,0:T(2,128)(2,1)} %param.12) | data formatting | bytes 262144 | tf_op jit(solution)/shard_map/reshape | solution.py:492
  2.3 0.7 copy.14
  3.0 87.2 %shard_map.109 = bf16[16,2,2048]{2,1,0:T(2,128)(2,1)} custom-call(s32[16]{0:T(128)} %select_reduce_fusion.holders, s32[1,64]{1,0:T(1,128)} %bitcast.13, s32[16]{0:T(128)} %lengths.1, bf16[16,32,128]{2,1,0:T(8,128)(2,1)} %bitcast.10, bf16[16,8,128]{2,1,0:T(8,128)(2,1)} %bitcast.11, bf16[64,2,2048]{2,1,0:T(2,128)(2,1)} %incoming.1, f32[1,2048]{1,0:T(1,128)} %bitcast.12, ...), custom_call_target="tpu_custom_call" | custom-call | tf_op jit(solution)/shard_map/pallas_call | solution.py:457
  90.2 1.7 %copy.17 = bf16[16,2,2048]{2,1,0:T(2,128)(2,1)} copy(bf16[16,2,2048]{2,1,0:T(2,128)(2,1)} %shard_map.109) | data formatting | bytes 262144
  (1 shorter events, 0.0 us)

commit v5 on v3

--- a/solution.py
+++ b/solution.py
@@ -216,13 +216,13 @@
     heads = T // HD
     chunks = groups // heads
     for g in range(kv_local):
-        @pl.loop(0, S // 4)
+        @pl.loop(0, S // 8)
         def _(j):
-            for n in range(4):
+            for n in range(8):
                 if g == 0:
-                    cache_copy(j * 4 + n).wait()
-            for n in range(4):
-                attend(j * 4 + n, g)
+                    cache_copy(j * 8 + n).wait()
+            for n in range(8):
+                attend(j * 8 + n, g)
 
         for k in range(chunks):
             for t in range(STEPS):

time: 91.9 us -> 91.5 us (level)
  no operation moved by 1% of the time
where the time goes in v5:
time: 91.5 us; the launch traced here: 91.3 us
  Pallas kernels  86.6 us (95%)
  local copies, waits for them, and re-layouts  3.32 us (4%)
  other arithmetic  1.34 us (1%)
    pallas_call x1, Pallas kernels, fused(): pl.pallas_call(functools.partial(layer_kernel, (Z, RB, T, NA, NF)), out_s...  86.6 us

profile of v5, /device:TPU:0, one launch (start us, length us, event | category | flops | bytes accessed | tf_op | source)
XLA Modules:
  0.0 91.3 jit_solution(12362239469077496201)
XLA Ops:
  0.0 1.3 %select_reduce_fusion.holders = s32[16]{0:T(128)} fusion(s32[64]{0:T(128)} %param.16, s32[16]{0:T(128)S(1)} %iota_add_fusion), kind=kLoop, calls=%fused_computation | loop fusion | flops 3056 | bytes 384 | tf_op jit(solution)/shard_map/reduce_sum | solution.py:487
  1.3 1.0 %reshape.17 = bf16[16,2,2,8,128]{4,3,2,1,0:T(8,128)(2,1)S(1)} reshape(bf16[16,2,2048]{2,1,0:T(2,128)(2,1)} %param.12) | data formatting | bytes 262144 | tf_op jit(solution)/shard_map/reshape | solution.py:481
  2.3 0.7 copy.14
  3.0 86.6 %shard_map.109 = bf16[16,2,2048]{2,1,0:T(2,128)(2,1)} custom-call(s32[16]{0:T(128)} %select_reduce_fusion.holders, s32[1,64]{1,0:T(1,128)} %bitcast.13, s32[16]{0:T(128)} %lengths.1, bf16[16,32,128]{2,1,0:T(8,128)(2,1)} %bitcast.10, bf16[16,8,128]{2,1,0:T(8,128)(2,1)} %bitcast.11, bf16[64,2,2048]{2,1,0:T(2,128)(2,1)} %incoming.1, f32[1,2048]{1,0:T(1,128)} %bitcast.12, ...), custom_call_target="tpu_custom_call" | custom-call | tf_op jit(solution)/shard_map/pallas_call | solution.py:447
  89.6 1.7 %copy.17 = bf16[16,2,2048]{2,1,0:T(2,128)(2,1)} copy(bf16[16,2,2048]{2,1,0:T(2,128)(2,1)} %shard_map.109) | data formatting | bytes 262144
  (1 shorter events, 0.0 us)
